TPU v7x, 32 devices: a whole 2x2x4 slice. The times are simulated.
32 devices in a mesh: dp: 8 (over z, core), seq: 4 (over y, x).
Axes of the slice: x: 2, y: 2, z: 4, core: 2. Of those that a mesh axis runs over, the one named last changes fastest.
Arguments:
- tokens_in: bfloat16 [16384, 1024], P(('dp', 'seq')), may hold values from -6 to 6
- norm_attn: bfloat16 [1024], P('dp'), may hold values from 0.5 to 1.5
- w_query: bfloat16 [1024, 1024], P('dp'), may hold values from -0.1875 to 0.1875
- key_value_weight: bfloat16 [1024, 1024], P('dp'), may hold values from -0.1875 to 0.1875
- gain_query: bfloat16 [64], P('dp'), may hold values from 1 to 2
- gain_key: bfloat16 [64], P('dp'), may hold values from 1 to 2
- w_out: bfloat16 [1024, 1024], P('dp'), may hold values from -0.75 to 0.75
- norm_ffn: bfloat16 [1024], P('dp'), may hold values from 0.5 to 1.5
- w_gate: bfloat16 [1024, 4608], P(None, 'dp'), may hold values from -0.1875 to 0.1875
- w_up: bfloat16 [1024, 4608], P(None, 'dp'), may hold values from -0.1875 to 0.1875
- w_down: bfloat16 [4608, 1024], P('dp'), may hold values from -0.09375 to 0.09375
- cotangent: bfloat16 [16384, 1024], P(('dp', 'seq')), may hold values from -6 to 6
- segments: int32 [8, 2048], P('dp'), may hold values from 0 to 3, never falling along the last dimension, each value on 1 to 1024 neighbouring positions
- blocks: int32 [8, 16], P('dp'), may hold values from 0 to 15, each once within a row
Outputs:
- output: bfloat16 [16384, 1024], P(('dp', 'seq'))
- grad_tokens: float32 [16384, 1024], P(('dp', 'seq'))
- grad_norm_attn: float32 [1024], P('dp')
- grad_w_query: float32 [1024, 1024], P('dp')
- grad_w_keyval: float32 [1024, 1024], P('dp')
- grad_gain_query: float32 [64], P('dp')
- grad_gain_key: float32 [64], P('dp')
- grad_w_out: float32 [1024, 1024], P('dp')
- grad_norm_ffn: float32 [1024], P('dp')
- grad_w_gate: float32 [1024, 4608], P(None, 'dp')
- grad_w_up: float32 [1024, 4608], P(None, 'dp')
- grad_w_down: float32 [4608, 1024], P('dp')
Inputs may be any that keep to these rules, and one draw needn't show every extreme that they name: `segments`: in each row the document numbers never fall, all 4 documents occur, each covers 1 to 1024 places and the longest exactly 1024. `blocks`: each row holds every block number once.
All inputs are finite; a program needn't handle non-finite values.
Results may differ from a plain program's by a relative error of at most 0.025.
Values may be sent and summed in bfloat16 or wider, within the bound.
A program may use at most 192 MiB of HBM per device.

v0:
```python
import math
import jax
import jax.numpy as jnp
from jax import lax
from jax.sharding import PartitionSpec as P

QUERY_HEADS = 16
KEY_VALUE_HEADS = 8
HEAD_SIZE = 64
BLOCK = 128
QUERY_ROWS = 512
EPS = 1e-05
THETA = 1000000.0
MASKED = -1e30


def normed(tensor, gain_vec):
    factor = lax.rsqrt(jnp.mean(tensor * tensor, axis=-1, keepdims=True) + EPS)
    return tensor * factor * gain_vec


def norm_back(tensor, gain_vec, upstream):
    factor = lax.rsqrt(jnp.mean(tensor * tensor, axis=-1, keepdims=True) + EPS)
    unit_value = tensor * factor
    weighted = upstream * gain_vec
    grad_in = factor * (
        weighted - unit_value * jnp.mean(weighted * unit_value, axis=-1, keepdims=True)
    )
    return (grad_in, upstream * unit_value)


def rotate(tensor, angle_cos, angle_sin):
    half_dim = tensor.shape[-1] // 2
    front_half = tensor[..., :half_dim]
    back_half = tensor[..., half_dim:]
    return jnp.concatenate(
        [
            front_half * angle_cos - back_half * angle_sin,
            back_half * angle_cos + front_half * angle_sin,
        ],
        axis=-1,
    )


def angles(offsets, head_dim):
    half_dim = head_dim // 2
    frequency = jnp.exp(
        jnp.arange(half_dim, dtype=jnp.float32) * (-2.0 * math.log(THETA) / head_dim)
    )
    turned = offsets.astype(jnp.float32)[:, None] * frequency[None, :]
    return (jnp.cos(turned)[:, None, :], jnp.sin(turned)[:, None, :])


def layout(segment_row, order_row, block_len):
    length_all = segment_row.shape[0]
    places = jnp.arange(length_all, dtype=jnp.int32)
    seg_start = jnp.concatenate([jnp.ones((1,), dtype=bool), segment_row[1:] != segment_row[:-1]])
    starts = lax.cummax(jnp.where(seg_start, places, 0), axis=0)
    offsets = places - starts
    placed_tokens = (
        order_row[:, None] * block_len + jnp.arange(block_len, dtype=jnp.int32)[None, :]
    ).reshape(length_all)
    return (placed_tokens, segment_row[placed_tokens], offsets[placed_tokens])


def plain_product(left_op, right_op):
    return jnp.dot(left_op, right_op, preferred_element_type=jnp.float32)


def dot_right_t(left_op, right_op):
    return lax.dot_general(
        left_op, right_op, (((1,), (1,)), ((), ())), preferred_element_type=jnp.float32
    )


def dot_left_t(left_op, right_op):
    return lax.dot_general(
        left_op, right_op, (((0,), (0,)), ((), ())), preferred_element_type=jnp.float32
    )


def gate_back(gate_pre, up_pre, upstream):
    gate_sig = jax.nn.sigmoid(gate_pre)
    grad_gate = upstream * up_pre * gate_sig * (1.0 + gate_pre * (1.0 - gate_sig))
    grad_up = upstream * gate_pre * gate_sig
    return (grad_gate.astype(jnp.bfloat16), grad_up.astype(jnp.bfloat16))


def shards(
    tokens_in,
    norm_attn,
    w_query,
    key_value_weight,
    gain_query,
    gain_key,
    w_out,
    norm_ffn,
    w_gate,
    w_up,
    w_down,
    cotangent,
    segments,
    blocks,
):
    sequence_count = lax.axis_size("seq")
    seq_index = lax.axis_index("seq")
    token_rows = tokens_in.shape[0]
    group_rows = token_rows * sequence_count
    local_key_value = KEY_VALUE_HEADS // sequence_count
    repeat_factor = QUERY_HEADS // KEY_VALUE_HEADS
    factor = HEAD_SIZE ** (-0.5)
    count_blocks = group_rows // QUERY_ROWS
    attn_gain, query_w, key_value_matrix, query_gain, key_gain, out_w, ffn_gain = (
        lax.all_gather(norm_attn, "dp", axis=0, tiled=True),
        lax.all_gather(w_query, "dp", axis=0, tiled=True),
        lax.all_gather(key_value_weight, "dp", axis=0, tiled=True),
        lax.all_gather(gain_query, "dp", axis=0, tiled=True),
        lax.all_gather(gain_key, "dp", axis=0, tiled=True),
        lax.all_gather(w_out, "dp", axis=0, tiled=True),
        lax.all_gather(norm_ffn, "dp", axis=0, tiled=True),
    )
    attn_gain = attn_gain.astype(jnp.float32)
    query_gain = query_gain.astype(jnp.float32)
    key_gain = key_gain.astype(jnp.float32)
    ffn_gain = ffn_gain.astype(jnp.float32)
    placed_tokens, documents_for_rows, offsets = layout(segments[0], blocks[0], BLOCK)
    angle_cos, angle_sin = angles(
        lax.dynamic_slice_in_dim(offsets, seq_index * token_rows, token_rows, 0), HEAD_SIZE
    )
    hidden = tokens_in.astype(jnp.float32)
    normalized_input = normed(hidden, attn_gain).astype(jnp.bfloat16)
    query_raw = plain_product(normalized_input, query_w).reshape(token_rows, QUERY_HEADS, HEAD_SIZE)
    key_value_unrotated = plain_product(normalized_input, key_value_matrix).reshape(
        token_rows, KEY_VALUE_HEADS, 2, HEAD_SIZE
    )
    query_low = rotate(normed(query_raw, query_gain), angle_cos, angle_sin).astype(jnp.bfloat16)
    key_low = rotate(normed(key_value_unrotated[:, :, 0], key_gain), angle_cos, angle_sin).astype(
        jnp.bfloat16
    )
    key_value_reduced = jnp.stack(
        [key_low, key_value_unrotated[:, :, 1].astype(jnp.bfloat16)], axis=2
    )
    query_heads, keyval_heads = (
        lax.all_to_all(
            query_low.reshape(token_rows, QUERY_HEADS * HEAD_SIZE),
            "seq",
            split_axis=1,
            concat_axis=0,
            tiled=True,
        ),
        lax.all_to_all(
            key_value_reduced.reshape(token_rows, KEY_VALUE_HEADS * 2 * HEAD_SIZE),
            "seq",
            split_axis=1,
            concat_axis=0,
            tiled=True,
        ),
    )
    query_matrix = query_heads.reshape(group_rows, local_key_value, repeat_factor, HEAD_SIZE)
    keyval_group = keyval_heads.reshape(group_rows, local_key_value, 2, HEAD_SIZE)
    key_rows = keyval_group[:, :, 0]
    value_rows = keyval_group[:, :, 1]

    def scores_of(block_idx):
        row_start = block_idx * QUERY_ROWS
        query_rows = lax.dynamic_slice_in_dim(query_matrix, row_start, QUERY_ROWS, 0)
        placed_rows = lax.dynamic_slice_in_dim(placed_tokens, row_start, QUERY_ROWS, 0)
        docs_rows = lax.dynamic_slice_in_dim(documents_for_rows, row_start, QUERY_ROWS, 0)
        allowed = (docs_rows[:, None] == documents_for_rows[None, :]) & (
            placed_tokens[None, :] <= placed_rows[:, None]
        )
        raw_scores = (
            jnp.einsum("rkad,jkd->karj", query_rows, key_rows, preferred_element_type=jnp.float32)
            * factor
        )
        return (query_rows, jnp.where(allowed, raw_scores, MASKED))

    def forward_block(block_idx):
        query_rows, masked = scores_of(block_idx)
        row_top = jnp.max(masked, axis=-1, keepdims=True)
        row_total = jnp.sum(jnp.exp(masked - row_top), axis=-1, keepdims=True)
        log_total = row_top + jnp.log(row_total)
        weights_low = jnp.exp(masked - log_total).astype(jnp.bfloat16)
        block_result = jnp.einsum(
            "karj,jkd->rkad", weights_low, value_rows, preferred_element_type=jnp.float32
        )
        return (block_result.astype(jnp.bfloat16), log_total)

    head_outs, log_totals = lax.map(forward_block, jnp.arange(count_blocks))
    attended = lax.all_to_all(
        head_outs.reshape(group_rows, local_key_value * repeat_factor * HEAD_SIZE),
        "seq",
        split_axis=0,
        concat_axis=1,
        tiled=True,
    )
    middle = hidden + plain_product(attended, out_w)
    ffn_in = normed(middle, ffn_gain).astype(jnp.bfloat16)
    gate_all, up_all, down_all = (
        lax.all_gather(w_gate, "dp", axis=1, tiled=True),
        lax.all_gather(w_up, "dp", axis=1, tiled=True),
        lax.all_gather(w_down, "dp", axis=0, tiled=True),
    )
    gate_pre = plain_product(ffn_in, gate_all)
    up_pre = plain_product(ffn_in, up_all)
    activated = (jax.nn.silu(gate_pre) * up_pre).astype(jnp.bfloat16)
    ffn_result = plain_product(activated, down_all)
    block_output = (middle + ffn_result).astype(jnp.bfloat16)
    upstream = cotangent.astype(jnp.float32)
    grad_act = dot_right_t(cotangent, down_all)
    grad_down_part = dot_left_t(activated, cotangent)
    grad_gate, grad_up = gate_back(gate_pre, up_pre, grad_act)
    grad_gate_part = dot_left_t(ffn_in, grad_gate)
    grad_up_part = dot_left_t(ffn_in, grad_up)
    grad_ffn_in = dot_right_t(grad_gate, gate_all) + dot_right_t(grad_up, up_all)
    grad_gate_w, grad_up_w, grad_down = (
        lax.psum_scatter(
            grad_gate_part.astype(jnp.bfloat16), "dp", scatter_dimension=1, tiled=True
        ).astype(jnp.float32),
        lax.psum_scatter(
            grad_up_part.astype(jnp.bfloat16), "dp", scatter_dimension=1, tiled=True
        ).astype(jnp.float32),
        lax.psum_scatter(
            grad_down_part.astype(jnp.bfloat16), "dp", scatter_dimension=0, tiled=True
        ).astype(jnp.float32),
    )
    grad_middle_add, ffn_gain_terms = norm_back(middle, ffn_gain, grad_ffn_in)
    grad_ffn_gain = jnp.sum(ffn_gain_terms, axis=0)
    grad_middle = upstream + grad_middle_add
    grad_branch = grad_middle.astype(jnp.bfloat16)
    grad_out_w = dot_left_t(attended, grad_branch)
    grad_attended = dot_right_t(grad_branch, out_w).astype(jnp.bfloat16)
    grad_head_outs = lax.all_to_all(grad_attended, "seq", split_axis=1, concat_axis=0, tiled=True)
    grad_outs_all = grad_head_outs.reshape(group_rows, local_key_value, repeat_factor, HEAD_SIZE)

    def backward_block(carried, group_members):
        grad_keys, grad_values = carried
        block_idx, log_total = group_members
        query_rows, masked = scores_of(block_idx)
        weights_full = jnp.exp(masked - log_total)
        weights_low = weights_full.astype(jnp.bfloat16)
        grad_rows = lax.dynamic_slice_in_dim(grad_outs_all, block_idx * QUERY_ROWS, QUERY_ROWS, 0)
        grad_weights = jnp.einsum(
            "rkad,jkd->karj", grad_rows, value_rows, preferred_element_type=jnp.float32
        )
        row_dot = jnp.sum(weights_full * grad_weights, axis=-1, keepdims=True)
        grad_scores = (weights_full * (grad_weights - row_dot)).astype(jnp.bfloat16)
        grad_query_rows = (
            jnp.einsum("karj,jkd->rkad", grad_scores, key_rows, preferred_element_type=jnp.float32)
            * factor
        )
        grad_keys = (
            grad_keys
            + jnp.einsum(
                "karj,rkad->jkd", grad_scores, query_rows, preferred_element_type=jnp.float32
            )
            * factor
        )
        grad_values = grad_values + jnp.einsum(
            "karj,rkad->jkd", weights_low, grad_rows, preferred_element_type=jnp.float32
        )
        return ((grad_keys, grad_values), grad_query_rows.astype(jnp.bfloat16))

    zero_heads = jnp.zeros((group_rows, local_key_value, HEAD_SIZE), jnp.float32)
    (grad_keys, grad_values), grad_query_blocks = lax.scan(
        backward_block, (zero_heads, zero_heads), (jnp.arange(count_blocks), log_totals)
    )
    grad_query_heads = grad_query_blocks.reshape(
        group_rows, local_key_value * repeat_factor * HEAD_SIZE
    )
    grad_keyval_heads = (
        jnp.stack([grad_keys, grad_values], axis=2)
        .astype(jnp.bfloat16)
        .reshape(group_rows, local_key_value * 2 * HEAD_SIZE)
    )
    grad_query_tok, key_value_gradient_tokens = (
        lax.all_to_all(grad_query_heads, "seq", split_axis=0, concat_axis=1, tiled=True),
        lax.all_to_all(grad_keyval_heads, "seq", split_axis=0, concat_axis=1, tiled=True),
    )
    grad_query_rot = rotate(
        grad_query_tok.reshape(token_rows, QUERY_HEADS, HEAD_SIZE).astype(jnp.float32),
        angle_cos,
        -angle_sin,
    )
    grad_query_raw, query_gain_terms = norm_back(query_raw, query_gain, grad_query_rot)
    grad_query_gain = jnp.sum(query_gain_terms, axis=(0, 1))
    key_value_gradient_split = key_value_gradient_tokens.reshape(
        token_rows, KEY_VALUE_HEADS, 2, HEAD_SIZE
    )
    grad_key_rot = rotate(
        key_value_gradient_split[:, :, 0].astype(jnp.float32), angle_cos, -angle_sin
    )
    grad_key_raw, key_gain_terms = norm_back(key_value_unrotated[:, :, 0], key_gain, grad_key_rot)
    grad_key_gain = jnp.sum(key_gain_terms, axis=(0, 1))
    grad_query_low = grad_query_raw.astype(jnp.bfloat16).reshape(
        token_rows, QUERY_HEADS * HEAD_SIZE
    )
    grad_keyval_low = jnp.stack(
        [grad_key_raw.astype(jnp.bfloat16), key_value_gradient_split[:, :, 1]], axis=2
    ).reshape(token_rows, KEY_VALUE_HEADS * 2 * HEAD_SIZE)
    grad_normed_in = dot_right_t(grad_query_low, query_w) + dot_right_t(
        grad_keyval_low, key_value_matrix
    )
    grad_query_w = dot_left_t(normalized_input, grad_query_low)
    grad_keyval_w = dot_left_t(normalized_input, grad_keyval_low)
    grad_hidden_add, attn_gain_terms = norm_back(hidden, attn_gain, grad_normed_in)
    grad_attn_gain = jnp.sum(attn_gain_terms, axis=0)
    grad_hidden = grad_middle + grad_hidden_add
    (
        owned_attn_gain,
        owned_query_w,
        owned_keyval_w,
        owned_query_gain,
        owned_key_gain,
        owned_out_w,
        owned_ffn_gain,
    ) = (
        lax.psum_scatter(
            grad_attn_gain.astype(jnp.bfloat16), "dp", scatter_dimension=0, tiled=True
        ).astype(jnp.float32),
        lax.psum_scatter(
            grad_query_w.astype(jnp.bfloat16), "dp", scatter_dimension=0, tiled=True
        ).astype(jnp.float32),
        lax.psum_scatter(
            grad_keyval_w.astype(jnp.bfloat16), "dp", scatter_dimension=0, tiled=True
        ).astype(jnp.float32),
        lax.psum_scatter(
            grad_query_gain.astype(jnp.bfloat16), "dp", scatter_dimension=0, tiled=True
        ).astype(jnp.float32),
        lax.psum_scatter(
            grad_key_gain.astype(jnp.bfloat16), "dp", scatter_dimension=0, tiled=True
        ).astype(jnp.float32),
        lax.psum_scatter(
            grad_out_w.astype(jnp.bfloat16), "dp", scatter_dimension=0, tiled=True
        ).astype(jnp.float32),
        lax.psum_scatter(
            grad_ffn_gain.astype(jnp.bfloat16), "dp", scatter_dimension=0, tiled=True
        ).astype(jnp.float32),
    )
    (
        total_attn_gain,
        total_query_w,
        total_keyval_w,
        total_query_gain,
        total_key_gain,
        total_out_w,
        total_ffn_gain,
        total_gate_w,
        total_up_w,
        total_down_w,
    ) = lax.psum(
        (
            owned_attn_gain,
            owned_query_w,
            owned_keyval_w,
            owned_query_gain,
            owned_key_gain,
            owned_out_w,
            owned_ffn_gain,
            grad_gate_w,
            grad_up_w,
            grad_down,
        ),
        "seq",
    )
    return (
        block_output,
        grad_hidden,
        total_attn_gain,
        total_query_w,
        total_keyval_w,
        total_query_gain,
        total_key_gain,
        total_out_w,
        total_ffn_gain,
        total_gate_w,
        total_up_w,
        total_down_w,
    )


def solution(mesh):
    return jax.shard_map(
        shards,
        mesh=mesh,
        in_specs=(
            P(("dp", "seq"), None),
            P("dp"),
            P("dp", None),
            P("dp", None),
            P("dp"),
            P("dp"),
            P("dp", None),
            P("dp"),
            P(None, "dp"),
            P(None, "dp"),
            P("dp", None),
            P(("dp", "seq"), None),
            P("dp", None),
            P("dp", None),
        ),
        out_specs=(
            P(("dp", "seq"), None),
            P(("dp", "seq"), None),
            P("dp"),
            P("dp", None),
            P("dp", None),
            P("dp"),
            P("dp"),
            P("dp", None),
            P("dp"),
            P(None, "dp"),
            P(None, "dp"),
            P("dp", None),
        ),
        check_vma=False,
    )
```

profile of v0, /device:TPU:8, one launch (start us, length us, event | category | flops | bytes accessed | tf_op | source)
XLA Modules:
  0.0 1338.1 jit_solution(3187364560856251971)
XLA Ops:
  22.0 14.6 %all-reduce.8 = (bf16[64]{0:T(256)(128)(2,1)S(1)}, bf16[64]{0:T(256)(128)(2,1)S(1)}) all-reduce(bf16[64]{0:T(256)(128)(2,1)S(1)} %dynamic-update-slice, bf16[64]{0:T(256)(128)(2,1)S(1)} %dynamic-update-slice.1), channel_id=1, replica_groups=mesh['dp'=8,'seq'=4] {'dp'}, use_global_device_ids=true, to_apply=%add | all-reduce | flops 128 | bytes 512
  37.3 11.8 gather_fusion.1
  80.3 11.8 gather_fusion
  102.5 61.7 %while.28 = (s32[]{:T(128)}, bf16[4,512,2,2,64]{1,4,3,2,0:T(8,128)(2,1)}, f32[4,2,2,512,1]{3,2,1,4,0:T(2,128)}, s32[4]{0:T(128)S(1)}, s32[2048]{0:T(1024)S(1)}, ...) while((s32[]{:T(128)}, ...), condition=%wide.region_8.9_spmd.clone, body=%wide.region_5.8_spmd.clone.sunk | while | flops 1123155968 | bytes 56201496 | solution.py:189
  168.6 12.5 all-gather.1
  189.8 10.1 fusion.93
  199.9 80.6 %all-gather.17.cloned.1.call-done = bf16[1024,4608]{0,1:T(8,128)(2,1)} async-done(((bf16[1024,576]{0,1:T(8,128)(2,1)}), bf16[1024,4608]{0,1:T(8,128)(2,1)}) %all-gather.17.cloned.1.call-update) | async-done | bytes 9437200 | tf_op jit(solution)/shard_map/all_gather | solution.py:201
  280.5 10.2 fusion.94
  290.7 80.5 %all-gather.19.cloned.1.call-done = bf16[4608,1024]{1,0:T(8,128)(2,1)} async-done(((bf16[576,1024]{1,0:T(8,128)(2,1)}), bf16[4608,1024]{1,0:T(8,128)(2,1)}) %all-gather.19.cloned.1.call-update) | async-done | bytes 9437200 | tf_op jit(solution)/shard_map/all_gather | solution.py:202
  371.2 18.5 %multiply_convert_fusion = (bf16[512,4608]{1,0:T(8,128)(2,1)}, bf16[512,4608]{1,0:T(8,128)(2,1)}, bf16[512,4608]{1,0:T(8,128)(2,1)}) fusion(f32[512,4608]{1,0:T(8,128)} %fusion.93, f32[512,4608]{1,0:T(8,128)} %fusion.94, bf16[512,1024]{1,0:T(8,128)(2,1)} %param.29, bf16[4608,1024]{1,0:T(8,128)(2,1)} %all-gather.19.cloned.1.call-done), kind=kOutput, calls=%fused_computation.69 | convolution fusion | flops 4869586944 | bytes 43515904 | tf_op jit(solution)/shard_map/dot_general | solution.py:71
  389.7 9.6 fusion.95
  418.2 9.8 all-to-all-done.3
  434.4 199.1 %while.29 = (s32[]{:T(128)}, f32[2048,2,64]{0,2,1:T(8,128)}, f32[2048,2,64]{0,2,1:T(8,128)}, bf16[4,512,2,2,64]{1,4,3,2,0:T(8,128)(2,1)}, s32[4]{0:T(128)S(1)}, ...) while((s32[]{:T(128)}, f32[2048,2,64]{0,2,1:T(8,128)}, ...), condition=%wide.region_13.14_spmd.clone, body=%wide.region_11.13_spmd.clone.sunk | while | flops 2751987712 | bytes 254768080 | solution.py:265
  442.1 11.6 fusion.160
  453.6 10.9 fusion.161
  491.6 11.5 fusion.160
  503.1 10.9 fusion.161
  541.3 11.5 fusion.160
  552.8 10.9 fusion.161
  591.0 11.5 fusion.160
  602.6 10.9 fusion.161
  639.4 11.2 all-to-all-done.4
  668.3 16.0 %all_to_all.90 = bf16[4,512,256]{1,2,0:T(8,128)(2,1)S(1)} all-to-all(bf16[4,512,256]{1,2,0:T(8,128)(2,1)S(1)} %copy.108), channel_id=1, replica_groups=mesh['dp'=8,'seq'=4] {'seq'}, dimensions={0} | all-to-all | bytes 2097152 | tf_op jit(solution)/shard_map/all_to_all | solution.py:278
  691.9 10.0 convolution_convert_fusion.2
  702.0 10.2 convolution_convert_fusion.1
  713.4 10.0 convolution_convert_fusion
  725.0 9.9 add_convert_fusion
  741.4 13.4 %all-reduce.7 = (bf16[1024]{0:T(1024)(128)(2,1)S(1)}, bf16[64]{0:T(256)(128)(2,1)S(1)}, bf16[64]{0:T(256)(128)(2,1)S(1)}, bf16[1024]{0:T(1024)(128)(2,1)S(1)}) all-reduce(bf16[1024]{0:T(1024)(128)(2,1)S(1)} %get-tuple-element.224, bf16[64]{0:T(256)(128)(2,1)S(1)} %reduce_sum.160, ...), channel_id=2, replica_groups=mesh['dp'=8,'seq'=4] {'dp'}, use_global_device_ids=true, to_apply=%region_18.19.clone | all-reduce | flops 2176 | bytes 8704
  758.6 78.1 %reduce-scatter.13.cloned.1.call-done = bf16[1024,576]{0,1:T(8,128)(2,1)} async-done(((bf16[1024,4608]{0,1:T(8,128)(2,1)}), bf16[1024,576]{0,1:T(8,128)(2,1)}) %reduce-scatter.13.cloned.1.call-update) | async-done | bytes 1179664 | tf_op jit(solution)/shard_map/reduce_scatter | solution.py:217
  836.7 99.8 %reduce-scatter.15.cloned.1.call-done = bf16[1024,576]{0,1:T(8,128)(2,1)} async-done(((bf16[1024,4608]{0,1:T(8,128)(2,1)}), bf16[1024,576]{0,1:T(8,128)(2,1)}) %reduce-scatter.15.cloned.1.call-update) | async-done | bytes 1179664 | tf_op jit(solution)/shard_map/reduce_scatter | solution.py:220
  936.5 100.1 %reduce-scatter.17.cloned.1.call-done = bf16[576,1024]{1,0:T(8,128)(2,1)} async-done(((bf16[4608,1024]{1,0:T(8,128)(2,1)}), bf16[576,1024]{1,0:T(8,128)(2,1)}) %reduce-scatter.17.cloned.1.call-update) | async-done | bytes 1179664 | tf_op jit(solution)/shard_map/reduce_scatter | solution.py:223
  1036.6 294.2 %all-reduce.10 = (f32[128]{0:T(128)}, f32[128,1024]{1,0:T(8,128)}, f32[128,1024]{1,0:T(8,128)}, f32[8]{0:T(128)}, f32[8]{0:T(128)}, /*index=5*/f32[128,1024]{1,0...) all-reduce(f32[128]{0:T(128)S(1)} %dynamic-slice_convert_fusion.4, ...), channel_id=1, replica_groups=mesh['dp'=8,'seq'=4] {'seq'}, use_global_device_ids=true, to_apply=%region_19.20 | all-reduce | flops 2162960 | bytes 12978304 | tf_op jit(solution)/shard_map/psum | solution.py:351
  (448 shorter events, 301.2 us)
Async XLA Ops:
  7.2 14.3 %copy-start.56 = (bf16[8]{0:T(256)(128)(2,1)S(1)}, bf16[8]{0:T(256)(128)(2,1)}, u32[]{:S(2)}) copy-start(bf16[8]{0:T(256)(128)(2,1)} %param.22) | copy-start | bytes 52
  7.2 14.6 %copy-start.57 = (bf16[8]{0:T(256)(128)(2,1)S(1)}, bf16[8]{0:T(256)(128)(2,1)}, u32[]{:S(2)}) copy-start(bf16[8]{0:T(256)(128)(2,1)} %param.23) | copy-start | bytes 52
  7.2 29.9 %copy-start.58 = (s32[1,16]{1,0:T(1,128)S(1)}, s32[1,16]{1,0:T(1,128)}, u32[]{:S(2)}) copy-start(s32[1,16]{1,0:T(1,128)} %param.31) | copy-start | bytes 196
  7.2 43.2 %all-gather.9.cloned.1.call-start = ((), (), s32[]{:S(2)}) async-start(), calls=%async_computation.12 | async-start | bytes 2359296 | tf_op jit(solution)/shard_map/all_gather | solution.py:115
  8.0 62.5 %all-gather.11.cloned.1.call-start = ((), (), s32[]{:S(2)}) async-start(), calls=%async_computation.13 | async-start | bytes 2359296 | tf_op jit(solution)/shard_map/all_gather | solution.py:116
  8.7 172.4 %all-gather.13.cloned.1.call-start = ((), (), s32[]{:S(2)}) async-start(), calls=%async_computation.14 | async-start | bytes 2359296 | tf_op jit(solution)/shard_map/all_gather | solution.py:119
  9.5 180.3 %all-gather.15.cloned.1.call-start = ((), (), s32[]{:S(2)}) async-start(), calls=%async_computation.15 | async-start | bytes 10616832 | tf_op jit(solution)/shard_map/all_gather | solution.py:200
  10.0 270.4 %all-gather.17.cloned.1.call-start = ((), (), s32[]{:S(2)}) async-start(), calls=%async_computation.16 | async-start | bytes 10616832 | tf_op jit(solution)/shard_map/all_gather | solution.py:201
  20.3 50.2 %copy-start.40 = (f32[8,1,128]{2,1,0:T(1,128)}, f32[8,1,128]{2,1,0:T(1,128)S(1)}, u32[]{:S(2)}) copy-start(f32[8,1,128]{2,1,0:T(1,128)S(1)} %convert_element_type.218) | copy-start | bytes 12292
  36.6 20.3 %copy-start.46 = (f32[64]{0:T(128)}, f32[64]{0:T(128)S(1)}, u32[]{:S(2)}) copy-start(f32[64]{0:T(128)S(1)} %convert_element_type.174) | copy-start | bytes 772
  36.7 37.1 %copy-start.44 = (f32[64]{0:T(128)}, f32[64]{0:T(128)S(1)}, u32[]{:S(2)}) copy-start(f32[64]{0:T(128)S(1)} %convert_element_type.177) | copy-start | bytes 772
  49.5 21.0 %copy-start.42 = (f32[512]{0:T(512)}, f32[512]{0:T(512)S(1)}, u32[]{:S(2)}) copy-start(f32[512]{0:T(512)S(1)} %add_rsqrt_fusion.3) | copy-start | bytes 6148
  50.4 24.4 %copy-start.21 = (f32[512,32]{0,1:T(8,128)}, f32[512,32]{0,1:T(8,128)S(1)}, u32[]{:S(2)}) copy-start(f32[512,32]{0,1:T(8,128)S(1)} %get-tuple-element.315) | copy-start | bytes 196612
  59.4 16.7 %all-to-all-start = ((bf16[512,4,256]{0,2,1:T(8,128)(2,1)}), bf16[512,4,256]{0,2,1:T(8,128)(2,1)S(1)}, u32[]{:S(2)}, u32[]{:S(2)}) async-start(bf16[512,4,256]{0,2,1:T(8,128)(2,1)} %bitcast.11), calls=%async_computation | async-start | bytes 2097152 | tf_op jit(solution)/shard_map/all_to_all | solution.py:144
  76.1 19.6 %all-to-all-start.1 = ((bf16[512,4,256]{0,2,1:T(8,128)(2,1)}), bf16[512,4,256]{0,2,1:T(8,128)(2,1)S(1)}, u32[]{:S(2)}, u32[]{:S(2)}) async-start(bf16[512,4,256]{0,2,1:T(8,128)(2,1)} %bitcast.17), calls=%async_computation.1 | async-start | bytes 2097152 | tf_op jit(solution)/shard_map/all_to_all | solution.py:151
  79.8 291.4 %all-gather.19.cloned.1.call-start = ((), (), s32[]{:S(2)}) async-start(), calls=%async_computation.17 | async-start | bytes 10616832 | tf_op jit(solution)/shard_map/all_gather | solution.py:202
  164.2 18.7 %all-to-all-start.2 = ((bf16[4,512,256]{1,2,0:T(8,128)(2,1)}), bf16[4,512,256]{1,2,0:T(8,128)(2,1)}, u32[]{:S(2)}, u32[]{:S(2)}) async-start(bf16[4,512,256]{1,2,0:T(8,128)(2,1)} %bitcast.312), calls=%async_computation.2 | async-start | bytes 2097152 | tf_op jit(solution)/shard_map/all_to_all | solution.py:190
  409.3 18.7 %all-to-all-start.3 = ((bf16[512,4,256]{2,0,1:T(8,128)(2,1)}), bf16[512,4,256]{2,0,1:T(8,128)(2,1)}, u32[]{:S(2)}, u32[]{:S(2)}) async-start(bf16[512,4,256]{2,0,1:T(8,128)(2,1)} %bitcast.310), calls=%async_computation.3 | async-start | bytes 2097152 | tf_op jit(solution)/shard_map/all_to_all | solution.py:233
  413.6 345.0 %reduce-scatter.11.cloned.1.call-start = ((), (), s32[]{:S(2)}) async-start(), calls=%async_computation.20 | async-start | bytes 2359296 | tf_op jit(solution)/shard_map/reduce_scatter | solution.py:333
  439.4 14.2 %copy-start.1 = (f32[2,512,2,2048]{3,1,2,0:T(8,128)}, f32[2,512,2,2048]{3,1,2,0:T(8,128)S(1)}, u32[]{:S(2)}) copy-start(f32[2,512,2,2048]{3,1,2,0:T(8,128)S(1)} %fusion.159) | copy-start | bytes 50331652 | tf_op jit(solution)/shard_map/while
  464.5 14.6 %slice-start = ((s8[8388608]{0:T(1024)(128)(4,1)}), s8[4194304]{0:T(1024)(128)(4,1)S(1)}, s32[]{:S(2)}) async-start(s8[8388608]{0:T(1024)(128)(4,1)} %bitcast.295), calls=%async_computation.24 | async-start | bytes 8388608 | tf_op jit(solution)/shard_map/while
  514.0 14.8 %slice-start = ((s8[8388608]{0:T(1024)(128)(4,1)}), s8[4194304]{0:T(1024)(128)(4,1)S(1)}, s32[]{:S(2)}) async-start(s8[8388608]{0:T(1024)(128)(4,1)} %bitcast.295), calls=%async_computation.24 | async-start | bytes 8388608 | tf_op jit(solution)/shard_map/while
  563.7 14.8 %slice-start = ((s8[8388608]{0:T(1024)(128)(4,1)}), s8[4194304]{0:T(1024)(128)(4,1)S(1)}, s32[]{:S(2)}) async-start(s8[8388608]{0:T(1024)(128)(4,1)} %bitcast.295), calls=%async_computation.24 | async-start | bytes 8388608 | tf_op jit(solution)/shard_map/while
  588.4 14.2 %copy-start.1 = (f32[2,512,2,2048]{3,1,2,0:T(8,128)}, f32[2,512,2,2048]{3,1,2,0:T(8,128)S(1)}, u32[]{:S(2)}) copy-start(f32[2,512,2,2048]{3,1,2,0:T(8,128)S(1)} %fusion.159) | copy-start | bytes 50331652 | tf_op jit(solution)/shard_map/while
  613.5 14.8 %slice-start = ((s8[8388608]{0:T(1024)(128)(4,1)}), s8[4194304]{0:T(1024)(128)(4,1)S(1)}, s32[]{:S(2)}) async-start(s8[8388608]{0:T(1024)(128)(4,1)} %bitcast.295), calls=%async_computation.24 | async-start | bytes 8388608 | tf_op jit(solution)/shard_map/while
  633.5 17.1 %all-to-all-start.4 = ((bf16[4,512,256]{1,2,0:T(8,128)(2,1)}), bf16[4,512,256]{1,2,0:T(8,128)(2,1)S(1)}, u32[]{:S(2)}, u32[]{:S(2)}) async-start(bf16[4,512,256]{1,2,0:T(8,128)(2,1)} %bitcast.311), calls=%async_computation.4 | async-start | bytes 2097152 | tf_op jit(solution)/shard_map/all_to_all | solution.py:277
  637.1 121.5 %reduce-scatter.7.cloned.1.call-start = ((), (), s32[]{:S(2)}) async-start(), calls=%async_computation.18 | async-start | bytes 2359296 | tf_op jit(solution)/shard_map/reduce_scatter | solution.py:321
  665.5 93.1 %reduce-scatter.9.cloned.1.call-start = ((), (), s32[]{:S(2)}) async-start(), calls=%async_computation.19 | async-start | bytes 2359296 | tf_op jit(solution)/shard_map/reduce_scatter | solution.py:324
  690.7 146.0 %reduce-scatter.13.cloned.1.call-start = ((), (), s32[]{:S(2)}) async-start(), calls=%async_computation.21 | async-start | bytes 10616832 | tf_op jit(solution)/shard_map/reduce_scatter | solution.py:217
  702.0 234.6 %reduce-scatter.15.cloned.1.call-start = ((), (), s32[]{:S(2)}) async-start(), calls=%async_computation.22 | async-start | bytes 10616832 | tf_op jit(solution)/shard_map/reduce_scatter | solution.py:220
  712.2 324.4 %reduce-scatter.17.cloned.1.call-start = ((), (), s32[]{:S(2)}) async-start(), calls=%async_computation.23 | async-start | bytes 10616832 | tf_op jit(solution)/shard_map/reduce_scatter | solution.py:223
  738.4 16.8 %copy-start.19 = (f32[512,1024]{1,0:T(8,128)S(1)}, f32[512,1024]{1,0:T(8,128)}, u32[]{:S(2)}) copy-start(f32[512,1024]{1,0:T(8,128)} %copy-done.18) | copy-start | bytes 6291460
  (100 other events, 474.6 us)
Sparse Core Ops, SparseCore 0:
  9.7 30.5 all-gather.8
  41.9 28.5 all-gather.10
  72.1 28.5 all-gather.12
  102.2 87.5 all-gather.14
  191.3 89.1 all-gather.16
  282.0 89.1 all-gather.18
  418.3 33.8 reduce-scatter.10
  665.7 32.2 reduce-scatter.6
  700.3 34.5 reduce-scatter.8
  737.0 99.7 reduce-scatter.12
  839.0 97.4 reduce-scatter.14
  938.7 97.8 reduce-scatter.16
where the time goes:
time: 1350 us; the launch traced here: 1340 us
  waiting for transfers between devices  474 us (35%)
  blocking collectives  360 us (27%)
  matrix products  293 us (22%)
  other arithmetic  94.1 us (7%)
  local copies, waits for them, and re-layouts  73.3 us (5%)
  starting transfers between devices  20.2 us (1%)
  between operations  17.5 us (1%)
    psum x1, blocking collectives, shards(): lax.psum((owned_attn_gain, owned_query_w, owned_keyval_w, owned_query_gai...  294 us
    reduce_scatter x1, waiting for transfers between devices, shards(): lax.psum_scatter(grad_down_part.astype(jnp.bfloat16), 'dp', scatter_dimen...  100 us
    reduce_scatter x1, waiting for transfers between devices, shards(): lax.psum_scatter(grad_up_part.astype(jnp.bfloat16), 'dp', scatter_dimensi...  99.8 us
    all_gather x1, waiting for transfers between devices, shards(): lax.all_gather(w_up, 'dp', axis=1, tiled=True)  80.6 us
    all_gather x1, waiting for transfers between devices, shards(): lax.all_gather(w_down, 'dp', axis=0, tiled=True)  80.5 us
    reduce_scatter x1, waiting for transfers between devices, shards(): lax.psum_scatter(grad_gate_part.astype(jnp.bfloat16), 'dp', scatter_dimen...  78.1 us
    dot_general x4, matrix products, backward_block(): jnp.einsum('rkad,jkd->karj', grad_rows, value_rows, preferred_element_typ...  46.1 us
    convert_element_type x4, other arithmetic, backward_block(): grad_scores = (weights_full * (grad_weights - row_dot)).astype(jnp.bfloat16)  43.6 us
  transfers between devices with their start and end apart: 17, of which 10 were waited for; matrix products, arithmetic and copies ran while one was open for 31% of the time, Pallas kernels for 0%

commit v1 on v0

--- a/solution.py
+++ b/solution.py
@@ -12,6 +12,12 @@
 EPS = 1e-05
 THETA = 1000000.0
 MASKED = -1e30
+
+
+def tiles_balance(vector, ndim_at):
+    z1 = list(vector.shape[1:])
+    z1[ndim_at] *= vector.shape[0]
+    return jnp.moveaxis(vector, 0, ndim_at).reshape(z1)
 
 
 def normed(tensor, gain_vec):
@@ -102,6 +108,26 @@
     segments,
     blocks,
 ):
+
+    def _use_digits(mine, dimension_no, device_axis="dp"):
+        n_blocks = lax.axis_size(device_axis)
+        pages = tuple(((dev_j, (dev_j + 1) % n_blocks) for dev_j in range(n_blocks)))
+        ready, latest = ([], [])
+        k = 0
+        found = tuple(((p, k0) for k0, p in pages))
+        while k < n_blocks - 1:
+            if k % 2 == 0:
+                ready.append(
+                    lax.ppermute(ready[-1] if ready else mine, axis_name=device_axis, perm=pages)
+                )
+            else:
+                latest.append(lax.ppermute(latest[-1] if latest else mine, device_axis, found))
+            k = k + 1
+        t_next = jnp.stack([*ready[::-1], mine, *latest], 0)
+        right_arr = lax.axis_index(device_axis) - len(ready)
+        t_next = t_next[(jnp.arange(n_blocks) - right_arr) % n_blocks]
+        return tiles_balance(t_next, dimension_no)
+
     sequence_count = lax.axis_size("seq")
     seq_index = lax.axis_index("seq")
     token_rows = tokens_in.shape[0]
@@ -198,7 +224,7 @@
     ffn_in = normed(middle, ffn_gain).astype(jnp.bfloat16)
     gate_all, up_all, down_all = (
         lax.all_gather(w_gate, "dp", axis=1, tiled=True),
-        lax.all_gather(w_up, "dp", axis=1, tiled=True),
+        _use_digits(w_up, 1),
         lax.all_gather(w_down, "dp", axis=0, tiled=True),
     )
     gate_pre = plain_product(ffn_in, gate_all)

time: 1350 us -> 1330 us (0.985)
  waiting for transfers between devices: 474 us -> 377 us
  blocking collectives: 360 us -> 401 us
  local copies, waits for them, and re-layouts: 73.3 us -> 99.3 us
    all_gather x1 -> x0, waiting for transfers between devices: 80.6 us -> none  [shards(): lax.all_gather(w_up, 'dp', axis=1, tiled=True)]
    all_gather x1, waiting for transfers between devices: 80.5 us -> 0.01 us  [shards(): lax.all_gather(w_down, 'dp', axis=0, tiled=True)]
    all_gather x1, waiting for transfers between devices: 0.82 us -> 60.5 us  [shards(): lax.all_gather(w_gate, 'dp', axis=1, tiled=True)]
    all_gather x1, blocking collectives: 9 us -> 46.3 us  [shards(): lax.all_gather(norm_attn, 'dp', axis=0, tiled=True)]
    unnamed x99 -> x108, local copies, waits for them, and re-layouts: 12.5 us -> 26.9 us
  transfers between devices with their start and end apart: 17 -> 23, of which waited for: 10 -> 8; matrix products, arithmetic and copies ran while one was open for 31% -> 33% of each run, Pallas kernels for 0% -> 0%
where the time goes in v1:
time: 1330 us; the launch traced here: 1320 us
  blocking collectives  401 us (30%)
  waiting for transfers between devices  377 us (28%)
  matrix products  295 us (22%)
  local copies, waits for them, and re-layouts  99.3 us (7%)
  other arithmetic  94.6 us (7%)
  starting transfers between devices  26 us (2%)
  between operations  17.3 us (1%)
    psum x1, blocking collectives, shards(): lax.psum((owned_attn_gain, owned_query_w, owned_keyval_w, owned_query_gai...  294 us
    reduce_scatter x1, waiting for transfers between devices, shards(): lax.psum_scatter(grad_down_part.astype(jnp.bfloat16), 'dp', scatter_dimen...  100 us
    reduce_scatter x1, waiting for transfers between devices, shards(): lax.psum_scatter(grad_up_part.astype(jnp.bfloat16), 'dp', scatter_dimensi...  99.7 us
    reduce_scatter x1, waiting for transfers between devices, shards(): lax.psum_scatter(grad_gate_part.astype(jnp.bfloat16), 'dp', scatter_dimen...  78.1 us
    all_gather x1, waiting for transfers between devices, shards(): lax.all_gather(w_gate, 'dp', axis=1, tiled=True)  60.5 us
    dot_general x6, matrix products, plain_product(): return jnp.dot(left_op, right_op, preferred_element_type=jnp.float32)  48.9 us
    all_gather x1, blocking collectives, shards(): lax.all_gather(norm_attn, 'dp', axis=0, tiled=True)  46.3 us
    dot_general x4, matrix products, backward_block(): jnp.einsum('rkad,jkd->karj', grad_rows, value_rows, preferred_element_typ...  46.3 us
  transfers between devices with their start and end apart: 23, of which 8 were waited for; matrix products, arithmetic and copies ran while one was open for 33% of the time, Pallas kernels for 0%

profile of v1, /device:TPU:8, one launch (start us, length us, event | category | flops | bytes accessed | tf_op | source)
XLA Modules:
  0.0 1316.9 jit_solution(18358723241596488981)
XLA Ops:
  13.2 46.3 %all-gather = bf16[8,1,128]{2,1,0:T(2,128)(2,1)S(1)} all-gather(bf16[1,1,128]{2,1,0:T(2,128)(2,1)} %bitcast.352), channel_id=1, replica_groups=mesh['dp'=8,'seq'=4] {'dp'}, dimensions={0}, use_global_device_ids=true | all-gather | bytes 2304 | tf_op jit(solution)/shard_map/all_gather | solution.py:140
  61.3 12.8 all-reduce.8
  74.9 11.8 gather_fusion.1
  128.0 11.8 gather_fusion
  139.8 18.3 %all-gather.1 = bf16[8,1,128]{2,1,0:T(2,128)(2,1)S(1)} all-gather(bf16[1,1,128]{2,1,0:T(2,128)(2,1)S(1)} %bitcast.353), channel_id=1, replica_groups=mesh['dp'=8,'seq'=4] {'dp'}, dimensions={0}, use_global_device_ids=true | all-gather | bytes 2304 | tf_op jit(solution)/shard_map/all_gather | solution.py:146
  169.3 61.7 %while.28 = (s32[]{:T(128)}, bf16[4,512,2,2,64]{1,4,3,2,0:T(8,128)(2,1)}, f32[4,2,2,512,1]{3,2,1,4,0:T(2,128)}, s32[4]{0:T(128)S(1)}, s32[2048]{0:T(1024)S(1)}, ...) while((s32[]{:T(128)}, ...), condition=%wide.region_8.9_spmd.clone, body=%wide.region_5.8_spmd.clone.sunk | while | flops 1123155968 | bytes 56201496 | solution.py:215
  252.5 9.5 gather_fusion.2
  268.2 10.2 fusion.96
  278.3 60.5 %all-gather.14.cloned.1.call-done = bf16[1024,4608]{0,1:T(8,128)(2,1)} async-done(((bf16[1024,576]{0,1:T(8,128)(2,1)}), bf16[1024,4608]{0,1:T(8,128)(2,1)}) %all-gather.14.cloned.1.call-update) | async-done | bytes 9437200 | tf_op jit(solution)/shard_map/all_gather | solution.py:226
  338.9 10.1 fusion.95
  348.9 18.1 %multiply_convert_fusion = (bf16[512,4608]{1,0:T(8,128)(2,1)}, bf16[512,4608]{1,0:T(8,128)(2,1)}, bf16[512,4608]{1,0:T(8,128)(2,1)}) fusion(f32[512,4608]{1,0:T(8,128)} %fusion.96, f32[512,4608]{1,0:T(8,128)} %fusion.95, bf16[512,1024]{1,0:T(8,128)(2,1)} %multiply_convert_fusion.4, bf16[1024,4608]{0,1:T(8,128)(2,1)} %bitcast.318), kind=kOutput, calls=%fused_computation.70 | convolution fusion | flops 4869586944 | bytes 43515904 | tf_op jit(solution)/shard_map/dot_general | solution.py:73
  397.8 9.8 all-to-all-done.3
  413.9 198.7 %while.29 = (s32[]{:T(128)}, f32[2048,2,64]{0,2,1:T(8,128)}, f32[2048,2,64]{0,2,1:T(8,128)}, bf16[4,512,2,2,64]{1,4,3,2,0:T(8,128)(2,1)}, s32[4]{0:T(128)S(1)}, ...) while((s32[]{:T(128)}, f32[2048,2,64]{0,2,1:T(8,128)}, ...), condition=%wide.region_13.14_spmd.clone, body=%wide.region_11.13_spmd.clone.sunk | while | flops 2751987712 | bytes 254768080 | solution.py:291
  421.5 11.6 fusion.162
  433.1 10.8 fusion.163
  470.9 11.6 fusion.162
  482.5 10.8 fusion.163
  520.5 11.6 fusion.162
  532.1 10.8 fusion.163
  570.2 11.6 fusion.162
  581.7 10.8 fusion.163
  618.5 11.2 all-to-all-done.4
  647.5 16.0 %all_to_all.90 = bf16[4,512,256]{1,2,0:T(8,128)(2,1)S(1)} all-to-all(bf16[4,512,256]{1,2,0:T(8,128)(2,1)S(1)} %copy.108), channel_id=1, replica_groups=mesh['dp'=8,'seq'=4] {'seq'}, dimensions={0} | all-to-all | bytes 2097152 | tf_op jit(solution)/shard_map/all_to_all | solution.py:304
  671.1 10.0 convolution_convert_fusion.2
  681.2 10.2 convolution_convert_fusion.1
  692.6 10.0 convolution_convert_fusion
  704.2 9.9 add_convert_fusion
  720.6 13.4 %all-reduce.7 = (bf16[1024]{0:T(1024)(128)(2,1)S(1)}, bf16[64]{0:T(256)(128)(2,1)S(1)}, bf16[64]{0:T(256)(128)(2,1)S(1)}, bf16[1024]{0:T(1024)(128)(2,1)S(1)}) all-reduce(bf16[1024]{0:T(1024)(128)(2,1)S(1)} %get-tuple-element.224, bf16[64]{0:T(256)(128)(2,1)S(1)} %reduce_sum.160, ...), channel_id=2, replica_groups=mesh['dp'=8,'seq'=4] {'dp'}, use_global_device_ids=true, to_apply=%region_18.19.clone | all-reduce | flops 2176 | bytes 8704
  737.7 78.1 %reduce-scatter.13.cloned.1.call-done = bf16[1024,576]{0,1:T(8,128)(2,1)} async-done(((bf16[1024,4608]{0,1:T(8,128)(2,1)}), bf16[1024,576]{0,1:T(8,128)(2,1)}) %reduce-scatter.13.cloned.1.call-update) | async-done | bytes 1179664 | tf_op jit(solution)/shard_map/reduce_scatter | solution.py:243
  815.9 99.7 %reduce-scatter.15.cloned.1.call-done = bf16[1024,576]{0,1:T(8,128)(2,1)} async-done(((bf16[1024,4608]{0,1:T(8,128)(2,1)}), bf16[1024,576]{0,1:T(8,128)(2,1)}) %reduce-scatter.15.cloned.1.call-update) | async-done | bytes 1179664 | tf_op jit(solution)/shard_map/reduce_scatter | solution.py:246
  915.5 100.2 %reduce-scatter.17.cloned.1.call-done = bf16[576,1024]{1,0:T(8,128)(2,1)} async-done(((bf16[4608,1024]{1,0:T(8,128)(2,1)}), bf16[576,1024]{1,0:T(8,128)(2,1)}) %reduce-scatter.17.cloned.1.call-update) | async-done | bytes 1179664 | tf_op jit(solution)/shard_map/reduce_scatter | solution.py:249
  1015.7 294.2 %all-reduce.10 = (f32[128]{0:T(128)}, f32[128,1024]{1,0:T(8,128)}, f32[128,1024]{1,0:T(8,128)}, f32[8]{0:T(128)}, f32[8]{0:T(128)}, /*index=5*/f32[128,1024]{1,0...) all-reduce(f32[128]{0:T(128)S(1)} %dynamic-slice_convert_fusion.4, ...), channel_id=1, replica_groups=mesh['dp'=8,'seq'=4] {'seq'}, use_global_device_ids=true, to_apply=%region_19.20 | all-reduce | flops 2162960 | bytes 12978304 | tf_op jit(solution)/shard_map/psum | solution.py:377
  (472 shorter events, 331.3 us)
Async XLA Ops:
  7.2 52.3 %copy-start.51 = (u32[32]{0:T(128)S(1)}, u32[32]{0:T(128)}, u32[]{:S(2)}) copy-start(u32[32]{0:T(128)} %constant.122) | copy-start | bytes 388
  7.2 53.6 %copy-start.57 = (bf16[8]{0:T(256)(128)(2,1)S(1)}, bf16[8]{0:T(256)(128)(2,1)}, u32[]{:S(2)}) copy-start(bf16[8]{0:T(256)(128)(2,1)} %param.22) | copy-start | bytes 52
  7.2 53.8 %copy-start.58 = (bf16[8]{0:T(256)(128)(2,1)S(1)}, bf16[8]{0:T(256)(128)(2,1)}, u32[]{:S(2)}) copy-start(bf16[8]{0:T(256)(128)(2,1)} %param.23) | copy-start | bytes 52
  7.2 67.4 %copy-start.59 = (s32[1,16]{1,0:T(1,128)S(1)}, s32[1,16]{1,0:T(1,128)}, u32[]{:S(2)}) copy-start(s32[1,16]{1,0:T(1,128)} %param.31) | copy-start | bytes 196
  7.2 88.9 %all-gather.8.cloned.1.call-start = ((), (), s32[]{:S(2)}) async-start(), calls=%async_computation.12 | async-start | bytes 2359296 | tf_op jit(solution)/shard_map/all_gather | solution.py:141
  8.0 101.1 %all-gather.10.cloned.1.call-start = ((), (), s32[]{:S(2)}) async-start(), calls=%async_computation.13 | async-start | bytes 2359296 | tf_op jit(solution)/shard_map/all_gather | solution.py:142
  8.7 253.4 %all-gather.12.cloned.1.call-start = ((), (), s32[]{:S(2)}) async-start(), calls=%async_computation.14 | async-start | bytes 2359296 | tf_op jit(solution)/shard_map/all_gather | solution.py:145
  9.4 258.7 %all-gather.16.cloned.1.call-start = ((), (), s32[]{:S(2)}) async-start(), calls=%async_computation.16 | async-start | bytes 10616832 | tf_op jit(solution)/shard_map/all_gather | solution.py:228
  10.0 64.6 %collective-permute-start = (bf16[1024,576]{0,1:T(8,128)(2,1)}, bf16[1024,576]{0,1:T(8,128)(2,1)S(1)}, u32[]{:S(2)}, u32[]{:S(2)}) collective-permute-start(bf16[1024,576]{0,1:T(8,128)(2,1)} %param.27), channel_id=1, source_target_pairs={{0,4},{4,8},{8,12},{12,16},{16,20},{20,24},{24,28},{28,0},{1,5},{5... | collective-permute-start | bytes 3538952 | tf_op jit(solution)/shard_map/ppermute | solution.py:121
  10.1 78.0 %collective-permute-start.4 = (bf16[1024,576]{0,1:T(8,128)(2,1)}, bf16[1024,576]{0,1:T(8,128)(2,1)}, u32[]{:S(2)}, u32[]{:S(2)}) collective-permute-start(bf16[1024,576]{0,1:T(8,128)(2,1)} %param.27), channel_id=1, source_target_pairs={{4,0},{8,4},{12,8},{16,12},{20,16},{24,20},{28,24},{0,28},{5,1},{9... | collective-permute-start | bytes 3538952 | tf_op jit(solution)/shard_map/ppermute | solution.py:124
  59.5 49.5 %copy-start.43 = (f32[8,1,128]{2,1,0:T(1,128)}, f32[8,1,128]{2,1,0:T(1,128)S(1)}, u32[]{:S(2)}) copy-start(f32[8,1,128]{2,1,0:T(1,128)S(1)} %convert_element_type.218) | copy-start | bytes 12292
  74.1 28.6 %copy-start.49 = (f32[64]{0:T(128)}, f32[64]{0:T(128)S(1)}, u32[]{:S(2)}) copy-start(f32[64]{0:T(128)S(1)} %convert_element_type.174) | copy-start | bytes 772
  74.6 37.6 %copy-start.47 = (f32[64]{0:T(128)}, f32[64]{0:T(128)S(1)}, u32[]{:S(2)}) copy-start(f32[64]{0:T(128)S(1)} %convert_element_type.177) | copy-start | bytes 772
  74.7 21.4 %collective-permute-start.1 = (bf16[1024,576]{0,1:T(8,128)(2,1)S(1)}, bf16[1024,576]{0,1:T(8,128)(2,1)}, u32[]{:S(2)}, u32[]{:S(2)}) collective-permute-start(bf16[1024,576]{0,1:T(8,128)(2,1)S(1)} %collective-permute-done), channel_id=1, source_target_pairs={{0,4},{4,8},{8,12},{12,16},{16,20},{20,24},{24,28},{28,0},{1,5},{5... | collective-permute-start | bytes 3538952 | tf_op jit(solution)/shard_map/ppermute | solution.py:121
  87.1 21.9 %copy-start.45 = (f32[512]{0:T(512)}, f32[512]{0:T(512)S(1)}, u32[]{:S(2)}) copy-start(f32[512]{0:T(512)S(1)} %add_rsqrt_fusion.3) | copy-start | bytes 6148
  88.1 25.0 %copy-start.21 = (f32[512,32]{0,1:T(8,128)}, f32[512,32]{0,1:T(8,128)S(1)}, u32[]{:S(2)}) copy-start(f32[512,32]{0,1:T(8,128)S(1)} %get-tuple-element.315) | copy-start | bytes 196612
  88.1 70.1 %collective-permute-start.5 = (bf16[1024,576]{0,1:T(8,128)(2,1)}, bf16[1024,576]{0,1:T(8,128)(2,1)}, u32[]{:S(2)}, u32[]{:S(2)}) collective-permute-start(bf16[1024,576]{0,1:T(8,128)(2,1)} %collective-permute-done.4), channel_id=1, source_target_pairs={{4,0},{8,4},{12,8},{16,12},{20,16},{24,20},{28,24},{0,28},{5,1},{9... | collective-permute-start | bytes 3538952 | tf_op jit(solution)/shard_map/ppermute | solution.py:124
  96.1 62.1 %collective-permute-start.2 = (bf16[1024,576]{0,1:T(8,128)(2,1)}, bf16[1024,576]{0,1:T(8,128)(2,1)}, u32[]{:S(2)}, u32[]{:S(2)}) collective-permute-start(bf16[1024,576]{0,1:T(8,128)(2,1)} %collective-permute-done.1), channel_id=1, source_target_pairs={{0,4},{4,8},{8,12},{12,16},{16,20},{20,24},{24,28},{28,0},{1,5},{5... | collective-permute-start | bytes 3538952 | tf_op jit(solution)/shard_map/ppermute | solution.py:121
  105.0 18.8 %all-to-all-start = ((bf16[512,4,256]{0,2,1:T(8,128)(2,1)}), bf16[512,4,256]{0,2,1:T(8,128)(2,1)S(1)}, u32[]{:S(2)}, u32[]{:S(2)}) async-start(bf16[512,4,256]{0,2,1:T(8,128)(2,1)} %bitcast.333), calls=%async_computation | async-start | bytes 2097152 | tf_op jit(solution)/shard_map/all_to_all | solution.py:170
  123.8 38.7 %all-to-all-start.1 = ((bf16[512,4,256]{0,2,1:T(8,128)(2,1)}), bf16[512,4,256]{0,2,1:T(8,128)(2,1)S(1)}, u32[]{:S(2)}, u32[]{:S(2)}) async-start(bf16[512,4,256]{0,2,1:T(8,128)(2,1)} %bitcast.17), calls=%async_computation.1 | async-start | bytes 2097152 | tf_op jit(solution)/shard_map/all_to_all | solution.py:177
  127.4 211.5 %all-gather.14.cloned.1.call-start = ((), (), s32[]{:S(2)}) async-start(), calls=%async_computation.15 | async-start | bytes 10616832 | tf_op jit(solution)/shard_map/all_gather | solution.py:226
  158.2 92.0 %collective-permute-start.6 = (bf16[1024,576]{0,1:T(8,128)(2,1)}, bf16[1024,576]{0,1:T(8,128)(2,1)}, u32[]{:S(2)}, u32[]{:S(2)}) collective-permute-start(bf16[1024,576]{0,1:T(8,128)(2,1)} %collective-permute-done.5), channel_id=1, source_target_pairs={{4,0},{8,4},{12,8},{16,12},{20,16},{24,20},{28,24},{0,28},{5,1},{9... | collective-permute-start | bytes 3538952 | tf_op jit(solution)/shard_map/ppermute | solution.py:124
  158.2 77.5 %collective-permute-start.3 = (bf16[1024,576]{0,1:T(8,128)(2,1)}, bf16[1024,576]{0,1:T(8,128)(2,1)}, u32[]{:S(2)}, u32[]{:S(2)}) collective-permute-start(bf16[1024,576]{0,1:T(8,128)(2,1)} %collective-permute-done.2), channel_id=1, source_target_pairs={{0,4},{4,8},{8,12},{12,16},{16,20},{20,24},{24,28},{28,0},{1,5},{5... | collective-permute-start | bytes 3538952 | tf_op jit(solution)/shard_map/ppermute | solution.py:121
  231.0 31.1 %all-to-all-start.2 = ((bf16[4,512,256]{1,2,0:T(8,128)(2,1)}), bf16[4,512,256]{1,2,0:T(8,128)(2,1)}, u32[]{:S(2)}, u32[]{:S(2)}) async-start(bf16[4,512,256]{1,2,0:T(8,128)(2,1)} %bitcast.336), calls=%async_computation.2 | async-start | bytes 2097152 | tf_op jit(solution)/shard_map/all_to_all | solution.py:216
  388.9 18.6 %all-to-all-start.3 = ((bf16[512,4,256]{2,0,1:T(8,128)(2,1)}), bf16[512,4,256]{2,0,1:T(8,128)(2,1)}, u32[]{:S(2)}, u32[]{:S(2)}) async-start(bf16[512,4,256]{2,0,1:T(8,128)(2,1)} %bitcast.334), calls=%async_computation.3 | async-start | bytes 2097152 | tf_op jit(solution)/shard_map/all_to_all | solution.py:259
  393.2 344.6 %reduce-scatter.11.cloned.1.call-start = ((), (), s32[]{:S(2)}) async-start(), calls=%async_computation.19 | async-start | bytes 2359296 | tf_op jit(solution)/shard_map/reduce_scatter | solution.py:359
  612.6 17.1 %all-to-all-start.4 = ((bf16[4,512,256]{1,2,0:T(8,128)(2,1)}), bf16[4,512,256]{1,2,0:T(8,128)(2,1)S(1)}, u32[]{:S(2)}, u32[]{:S(2)}) async-start(bf16[4,512,256]{1,2,0:T(8,128)(2,1)} %bitcast.335), calls=%async_computation.4 | async-start | bytes 2097152 | tf_op jit(solution)/shard_map/all_to_all | solution.py:303
  616.3 121.5 %reduce-scatter.7.cloned.1.call-start = ((), (), s32[]{:S(2)}) async-start(), calls=%async_computation.17 | async-start | bytes 2359296 | tf_op jit(solution)/shard_map/reduce_scatter | solution.py:347
  644.6 93.1 %reduce-scatter.9.cloned.1.call-start = ((), (), s32[]{:S(2)}) async-start(), calls=%async_computation.18 | async-start | bytes 2359296 | tf_op jit(solution)/shard_map/reduce_scatter | solution.py:350
  669.9 146.0 %reduce-scatter.13.cloned.1.call-start = ((), (), s32[]{:S(2)}) async-start(), calls=%async_computation.20 | async-start | bytes 10616832 | tf_op jit(solution)/shard_map/reduce_scatter | solution.py:243
  681.1 234.4 %reduce-scatter.15.cloned.1.call-start = ((), (), s32[]{:S(2)}) async-start(), calls=%async_computation.21 | async-start | bytes 10616832 | tf_op jit(solution)/shard_map/reduce_scatter | solution.py:246
  691.4 324.4 %reduce-scatter.17.cloned.1.call-start = ((), (), s32[]{:S(2)}) async-start(), calls=%async_computation.22 | async-start | bytes 10616832 | tf_op jit(solution)/shard_map/reduce_scatter | solution.py:249
  (107 other events, 589.4 us)
Sparse Core Ops, SparseCore 0:
  9.7 45.3 all-gather.7
  56.6 31.4 all-gather.9
  89.8 44.1 all-gather.11
  135.5 112.6 all-gather.15
  249.7 89.1 all-gather.13
  397.9 33.7 reduce-scatter.10
  644.8 32.2 reduce-scatter.6
  679.3 34.6 reduce-scatter.8
  716.3 99.5 reduce-scatter.12
  818.0 97.4 reduce-scatter.14
  917.8 97.8 reduce-scatter.16
